TPU v7x, 32 devices: a whole 2x2x4 slice. The times are simulated.
32 devices in a mesh: img: 4 (over y, x), tpl: 8 (over z, core).
Axes of the slice: x: 2, y: 2, z: 4, core: 2. Of those that a mesh axis runs over, the one named last changes fastest.
Arguments:
- images: bfloat16 [6144, 2048], P(('img', 'tpl')), may hold values from -320 to 320
- templates: bfloat16 [3072, 2048], P('tpl'), may hold values from -0.62 to 0.62
- class_exponent: int32 [8], replicated, may hold values from 0 to 5
- class_mask: int32 [6144, 8], P('img'), may hold values from 0 to 1, as said below
Outputs:
- new_templates: float32 [3072, 2048], P('tpl', 'img')
- log_evidence: float32 [6144], P('img')
Inputs may be any that keep to these rules, and one draw needn't show every extreme that they name: `class_mask`: every image is compared with at least one class.
All inputs are finite; a program needn't handle non-finite values.
Results may differ from a plain program's by a relative error of at most 0.0023.
Values may be sent and summed in bfloat16 or wider, within the bound.
A program may use at most 64 MiB of HBM per device.

v0:
```python
import jax
import jax.numpy as jnp
from jax import lax
from jax.sharding import PartitionSpec as P

floor_score = -1e30


def per_device(images, templates, class_exponent, class_mask):
    tpl_rows = templates.shape[0]
    feature_count = templates.shape[1]
    class_count = class_exponent.shape[0]
    per_class = tpl_rows * lax.axis_size("tpl") // class_count
    global_rows = lax.axis_index("tpl") * tpl_rows + jnp.arange(tpl_rows, dtype=jnp.int32)
    owner = global_rows // per_class
    onehot = (jnp.arange(class_count, dtype=jnp.int32)[:, None] == owner[None, :]).astype(
        jnp.float32
    )
    inverse_temp = 0.5 * jnp.exp2(0.5 * class_exponent.astype(jnp.float32))
    template_beta = jnp.sum(onehot * inverse_temp[:, None], axis=0)
    allowed = jnp.dot(class_mask.astype(jnp.float32), onehot, precision=lax.Precision.HIGHEST) > 0.5
    squared_norm = jnp.sum(jnp.square(templates.astype(jnp.float32)), axis=1)
    gathered = lax.all_gather(images, "tpl", axis=0, tiled=True)
    raw = lax.dot_general(
        gathered, templates, (((1,), (1,)), ((), ())), preferred_element_type=jnp.float32
    )
    scores = template_beta[None, :] * (raw - 0.5 * squared_norm[None, :])
    local_top = jnp.max(jnp.where(allowed, scores, floor_score), axis=1)
    top = lax.pmax(local_top, "tpl")
    expo = jnp.where(allowed, jnp.exp(scores - top[:, None]), 0.0)
    totals = lax.psum(jnp.sum(expo, axis=1), "tpl")
    posterior = expo / totals[:, None]
    posterior_bf = posterior.astype(jnp.bfloat16)
    occupancy_part = jnp.sum(posterior, axis=0)
    weighted_part = lax.dot_general(
        posterior_bf, gathered, (((0,), (0,)), ((), ())), preferred_element_type=jnp.float32
    )
    columns = feature_count // lax.axis_size("img")
    col_start = lax.axis_index("img") * columns
    own_share = lax.psum_scatter(weighted_part, "img", scatter_dimension=1, tiled=True)
    occupancy = lax.psum(occupancy_part, "img")
    own_templates = lax.dynamic_slice_in_dim(templates, col_start, columns, 1).astype(jnp.float32)
    new_templates = (own_share + own_templates) / (occupancy[:, None] + 1.0)
    log_evidence = top + jnp.log(totals)
    return (new_templates, log_evidence)


def solution(mesh):
    in_specs = (P(("img", "tpl"), None), P("tpl", None), P(), P("img", None))
    out_specs = (P("tpl", "img"), P("img"))
    return jax.shard_map(
        per_device, mesh=mesh, in_specs=in_specs, out_specs=out_specs, check_vma=False
    )
```

profile of v0, /device:TPU:0, one launch (start us, length us, event | category | flops | bytes accessed | tf_op | source)
XLA Modules:
  0.0 171.4 jit_solution(5243481778394577077)
XLA Ops:
  7.2 0.0 all-gather.2.cloned.1.call-start
  7.2 0.7 all-gather.2.cloned.1.call-update
  7.9 0.0 reduce-scatter.2.cloned.1.call-start
  8.0 0.7 exponential_multiply_fusion
  8.6 0.1 select_reduce_fusion.1
  8.7 1.8 %multiply_reduce_fusion = f32[384]{0:T(512)S(1)} fusion(bf16[384,2048]{1,0:T(8,128)(2,1)} %param.5), kind=kLoop, calls=%fused_computation | loop fusion | flops 2358912 | bytes 1574400 | tf_op jit(solution)/shard_map/reduce_sum | solution.py:22
  10.5 0.0 copy-start
  10.5 66.5 %all-gather.2.cloned.1.call-done = bf16[1536,2048]{1,0:T(8,128)(2,1)} async-done(((bf16[192,2048]{1,0:T(8,128)(2,1)}), bf16[1536,2048]{1,0:T(8,128)(2,1)}) %all-gather.2.cloned.1.call-update) | async-done | bytes 6291472 | tf_op jit(solution)/shard_map/all_gather | solution.py:23
  77.1 5.2 %fusion = f32[1536,384]{0,1:T(8,128)S(1)} fusion(bf16[1536,2048]{1,0:T(8,128)(2,1)} %all-gather.2.cloned.1.call-done, bf16[384,2048]{1,0:T(8,128)(2,1)} %param.5, f32[384]{0:T(512)S(1)} %broadcast_multiply_fusion, f32[384]{0:T(512)S(1)} %select_reduce_fusion.1), kind=kOutput, calls=%fused_computation.2 | convolution fusion | flops 2417098752 | bytes 10226688 | tf_op jit(solution)/shard_map/dot_general | solution.py:24
  82.3 0.0 copy-done
  82.3 1.5 select_reduce_fusion
  83.8 14.4 %pmax.7 = f32[1536]{0:T(1024)S(1)} all-reduce(f32[1536]{0:T(1024)S(1)} %get-tuple-element.2), channel_id=1, replica_groups=mesh['img'=4,'tpl'=8] {'tpl'}, use_global_device_ids=true, to_apply=%region_3.4 | all-reduce | flops 1536 | bytes 12288 | tf_op jit(solution)/shard_map/pmax | solution.py:29
  98.3 0.6 fusion.3
  98.8 13.9 %psum.14 = f32[1536]{0:T(1024)S(1)} all-reduce(f32[1536]{0:T(1024)S(1)} %fusion.3), channel_id=1, replica_groups=mesh['img'=4,'tpl'=8] {'tpl'}, use_global_device_ids=true, to_apply=%region_5.6 | all-reduce | flops 1536 | bytes 12288 | tf_op jit(solution)/shard_map/psum | solution.py:31
  112.8 7.1 %fusion.4 = f32[384,2048]{1,0:T(8,128)} fusion(bf16[1536,2048]{1,0:T(8,128)(2,1)} %all-gather.2.cloned.1.call-done, pred[1536,384]{0,1:T(32,128)(4,1)S(1)} %get-tuple-element.3, f32[1536,384]{0,1:T(8,128)S(1)} %fusion, f32[1536]{0:T(1024)S(1)} %psum.14, f32[1536]{0:T(1024)S(1)} %pmax.7), kind=kOutput, calls=%fused_computation.9 | convolution fusion | flops 2418278400 | bytes 12398592 | tf_op jit(solution)/shard_map/dot_general | solution.py:35
  119.9 0.0 reduce-scatter.2.cloned.1.call-update
  119.9 0.7 fusion.6
  120.6 10.4 %psum.15 = f32[384]{0:T(512)S(1)} all-reduce(f32[384]{0:T(512)S(1)} %fusion.6), channel_id=1, replica_groups=mesh['img'=4,'tpl'=8] {'img'}, use_global_device_ids=true, to_apply=%region_8.9 | all-reduce | flops 384 | bytes 3072 | tf_op jit(solution)/shard_map/psum | solution.py:41
  131.0 0.6 log_add_fusion
  131.6 30.7 %reduce-scatter.2.cloned.1.call-done = f32[384,512]{1,0:T(8,128)} async-done(((f32[384,2048]{1,0:T(8,128)}), f32[384,512]{1,0:T(8,128)}) %reduce-scatter.2.cloned.1.call-update) | async-done | bytes 786448 | tf_op jit(solution)/shard_map/reduce_scatter | solution.py:40
  162.3 2.2 %add_divide_fusion = f32[384,512]{1,0:T(8,128)} fusion(f32[384,512]{1,0:T(8,128)} %reduce-scatter.2.cloned.1.call-done, f32[384]{0:T(512)S(1)} %broadcast_add_fusion, bf16[384,2048]{1,0:T(8,128)(2,1)} %param.5, s32[]{:T(128)S(6)} %select_n.22), kind=kLoop, calls=%fused_computation.11 | loop fusion | flops 589824 | bytes 1967620 | tf_op jit(solution)/shard_map/div | solution.py:43
  (3 shorter events, 0.0 us)
Async XLA Ops:
  7.2 69.9 %all-gather.2.cloned.1.call-start = ((), (), s32[]{:S(2)}) async-start(), calls=%async_computation.1 | async-start | bytes 7077888 | tf_op jit(solution)/shard_map/all_gather | solution.py:23
  7.9 154.4 %reduce-scatter.2.cloned.1.call-start = ((), (), s32[]{:S(2)}) async-start(), calls=%async_computation.2 | async-start | bytes 3932160 | tf_op jit(solution)/shard_map/reduce_scatter | solution.py:40
  10.5 71.8 %copy-start = (s32[1536,8]{0,1:T(8,128)S(1)}, s32[1536,8]{0,1:T(8,128)}, u32[]{:S(2)}) copy-start(s32[1536,8]{0,1:T(8,128)} %param.7) | copy-start | bytes 147460
Sparse Core Ops, SparseCore 0:
  9.6 67.4 all-gather.1
  120.0 42.2 reduce-scatter.1
where the time goes:
time: 172 us; the launch traced here: 171 us
  waiting for transfers between devices  97.9 us (57%)
  blocking collectives  38.7 us (23%)
  between operations  14.1 us (8%)
  matrix products  13.9 us (8%)
  other arithmetic  6.69 us (4%)
    all_gather x1, waiting for transfers between devices, per_device(): gathered = lax.all_gather(images, 'tpl', axis=0, tiled=True)  66.5 us
    reduce_scatter x1, waiting for transfers between devices, per_device(): lax.psum_scatter(weighted_part, 'img', scatter_dimension=1, tiled=True)  30.7 us
    pmax x1, blocking collectives, per_device(): top = lax.pmax(local_top, 'tpl')  14.4 us
    psum x1, blocking collectives, per_device(): totals = lax.psum(jnp.sum(expo, axis=1), 'tpl')  13.9 us
    psum x1, blocking collectives, per_device(): occupancy = lax.psum(occupancy_part, 'img')  10.4 us
    dot_general x1, matrix products, per_device(): lax.dot_general(posterior_bf, gathered, (((0,), (0,)), ((), ())), preferr...  7.11 us
    dot_general x1, matrix products, per_device(): lax.dot_general(gathered, templates, (((1,), (1,)), ((), ())), preferred_...  5.24 us
  transfers between devices with their start and end apart: 2, of which 2 were waited for; matrix products, arithmetic and copies ran while one was open for 2% of the time, Pallas kernels for 0%

commit v1 on v0

--- a/solution.py
+++ b/solution.py
@@ -4,6 +4,19 @@
 from jax.sharding import PartitionSpec as P
 
 floor_score = -1e30
+
+
+def gather_around(x, axis, dim):
+    ways = lax.axis_size(axis)
+    up = [(d, (d + 1) % ways) for d in range(ways)]
+    down = [(d, (d - 1) % ways) for d in range(ways)]
+    earlier, later = ([x], [x])
+    for _ in range(ways // 2):
+        earlier.append(lax.ppermute(earlier[-1], axis, up))
+    for _ in range((ways - 1) // 2):
+        later.append(lax.ppermute(later[-1], axis, down))
+    line = jnp.concatenate([*earlier[::-1], *later[1:]], axis=dim)
+    return jnp.roll(line, (lax.axis_index(axis) - ways // 2) * x.shape[dim], axis=dim)
 
 
 def per_device(images, templates, class_exponent, class_mask):
@@ -20,7 +33,7 @@
     template_beta = jnp.sum(onehot * inverse_temp[:, None], axis=0)
     allowed = jnp.dot(class_mask.astype(jnp.float32), onehot, precision=lax.Precision.HIGHEST) > 0.5
     squared_norm = jnp.sum(jnp.square(templates.astype(jnp.float32)), axis=1)
-    gathered = lax.all_gather(images, "tpl", axis=0, tiled=True)
+    gathered = gather_around(images, "tpl", 0)
     raw = lax.dot_general(
         gathered, templates, (((1,), (1,)), ((), ())), preferred_element_type=jnp.float32
     )

time: 172 us -> 187 us (1.087)
  starting transfers between devices: 0.08 us -> 11.3 us
  local copies, waits for them, and re-layouts: 0.01 us -> 9.31 us
  waiting for transfers between devices: 97.9 us -> 93.9 us
  matrix products: 13.9 us -> 11.7 us
    all_gather x1 -> x0, waiting for transfers between devices: 66.5 us -> none  [per_device(): gathered = lax.all_gather(images, 'tpl', axis=0, tiled=True)]
    ppermute x0 -> x7, waiting for transfers between devices: none -> 63.2 us  [the longest x4 63.2 us: gather_around(): earlier.append(lax.ppermute(earlier[-1], axis, up))]
    ppermute x0 -> x7, starting transfers between devices: none -> 11.2 us  [the longest x3 10.7 us: gather_around(): later.append(lax.ppermute(later[-1], axis, down))]
    unnamed x2 -> x23, local copies, waits for them, and re-layouts: 0.01 us -> 9.24 us
    dot_general x1, matrix products: 5.24 us -> 2.66 us  [per_device(): lax.dot_general(gathered, templates, (((1,), (1,)), ((), ())), preferred_...]
  transfers between devices with their start and end apart: 2 -> 8, of which waited for: 2 -> 5; matrix products, arithmetic and copies ran while one was open for 2% -> 5% of each run, Pallas kernels for 0% -> 0%
where the time goes in v1:
time: 187 us; the launch traced here: 186 us
  waiting for transfers between devices  93.9 us (50%)
  blocking collectives  38.9 us (21%)
  between operations  14.3 us (8%)
  matrix products  11.7 us (6%)
  starting transfers between devices  11.3 us (6%)
  local copies, waits for them, and re-layouts  9.31 us (5%)
  other arithmetic  6.69 us (4%)
    ppermute x4, waiting for transfers between devices, gather_around(): earlier.append(lax.ppermute(earlier[-1], axis, up))  63.2 us
    reduce_scatter x1, waiting for transfers between devices, per_device(): lax.psum_scatter(weighted_part, 'img', scatter_dimension=1, tiled=True)  30.7 us
    psum x1, blocking collectives, per_device(): totals = lax.psum(jnp.sum(expo, axis=1), 'tpl')  13.9 us
    pmax x1, blocking collectives, per_device(): top = lax.pmax(local_top, 'tpl')  13.9 us
    psum x1, blocking collectives, per_device(): occupancy = lax.psum(occupancy_part, 'img')  11.1 us
    ppermute x3, starting transfers between devices, gather_around(): later.append(lax.ppermute(later[-1], axis, down))  10.7 us
    unnamed x23, local copies, waits for them, and re-layouts  9.24 us
    dot_general x1, matrix products, per_device(): lax.dot_general(posterior_bf, gathered, (((0,), (0,)), ((), ())), preferr...  7.48 us
  transfers between devices with their start and end apart: 8, of which 5 were waited for; matrix products, arithmetic and copies ran while one was open for 5% of the time, Pallas kernels for 0%

profile of v1, /device:TPU:0, one launch (start us, length us, event | category | flops | bytes accessed | tf_op | source)
XLA Modules:
  0.0 186.0 jit_solution(7643583923374049066)
XLA Ops:
  7.2 0.0 copy-start
  7.2 0.0 reduce-scatter.2.cloned.1.call-start
  7.2 0.5 collective-permute-start
  7.8 13.9 %collective-permute-done = bf16[192,2048]{1,0:T(8,128)(2,1)S(1)} collective-permute-done((bf16[192,2048]{1,0:T(8,128)(2,1)}, bf16[192,2048]{1,0:T(8,128)(2,1)S(1)}, u32[]{:S(2)}, u32[]{:S(2)}) %collective-permute-start) | collective-permute-done | bytes 786464 | tf_op jit(solution)/shard_map/ppermute | solution.py:15
  21.7 0.0 collective-permute-start.1
  21.7 3.5 %collective-permute-start.4 = (bf16[192,2048]{1,0:T(8,128)(2,1)}, bf16[192,2048]{1,0:T(8,128)(2,1)S(1)}, u32[]{:S(2)}, u32[]{:S(2)}) collective-permute-start(bf16[192,2048]{1,0:T(8,128)(2,1)} %param.4), channel_id=1, source_target_pairs={{0,7},{1,0},{2,1},{3,2},{4,3},{5,4},{6,5},{7,6},{8,15},{9,8},{10,9... | collective-permute-start | bytes 2359304 | tf_op jit(solution)/shard_map/ppermute | solution.py:17
  25.2 17.2 %collective-permute-done.1 = bf16[192,2048]{1,0:T(8,128)(2,1)S(1)} collective-permute-done((bf16[192,2048]{1,0:T(8,128)(2,1)S(1)}, bf16[192,2048]{1,0:T(8,128)(2,1)S(1)}, u32[]{:S(2)}, u32[]{:S(2)}) %collective-permute-start.1) | collective-permute-done | bytes 786464 | tf_op jit(solution)/shard_map/ppermute | solution.py:15
  42.4 0.0 collective-permute-start.2
  42.4 0.0 collective-permute-done.4
  42.4 3.5 %collective-permute-start.5 = (bf16[192,2048]{1,0:T(8,128)(2,1)S(1)}, bf16[192,2048]{1,0:T(8,128)(2,1)}, u32[]{:S(2)}, u32[]{:S(2)}) collective-permute-start(bf16[192,2048]{1,0:T(8,128)(2,1)S(1)} %collective-permute-done.4), channel_id=1, source_target_pairs={{0,7},{1,0},{2,1},{3,2},{4,3},{5,4},{6,5},{7,6},{8,15},{9,8},{10,9... | collective-permute-start | bytes 2359304 | tf_op jit(solution)/shard_map/ppermute | solution.py:17
  45.9 17.5 %collective-permute-done.2 = bf16[192,2048]{1,0:T(8,128)(2,1)} collective-permute-done((bf16[192,2048]{1,0:T(8,128)(2,1)S(1)}, bf16[192,2048]{1,0:T(8,128)(2,1)}, u32[]{:S(2)}, u32[]{:S(2)}) %collective-permute-start.2) | collective-permute-done | bytes 786464 | tf_op jit(solution)/shard_map/ppermute | solution.py:15
  63.4 0.0 collective-permute-start.3
  63.5 0.7 exponential_multiply_fusion
  64.1 0.1 select_reduce_fusion.1
  64.2 1.8 multiply_reduce_fusion
  66.0 0.0 copy-start.1
  66.0 0.0 collective-permute-done.5
  66.0 3.6 %collective-permute-start.6 = (bf16[192,2048]{1,0:T(8,128)(2,1)}, bf16[192,2048]{1,0:T(8,128)(2,1)S(1)}, u32[]{:S(2)}, u32[]{:S(2)}) collective-permute-start(bf16[192,2048]{1,0:T(8,128)(2,1)} %collective-permute-done.5), channel_id=1, source_target_pairs={{0,7},{1,0},{2,1},{3,2},{4,3},{5,4},{6,5},{7,6},{8,15},{9,8},{10,9... | collective-permute-start | bytes 2359304 | tf_op jit(solution)/shard_map/ppermute | solution.py:17
  69.6 14.6 %collective-permute-done.3 = bf16[192,2048]{1,0:T(8,128)(2,1)} collective-permute-done((bf16[192,2048]{1,0:T(8,128)(2,1)}, bf16[192,2048]{1,0:T(8,128)(2,1)}, u32[]{:S(2)}, u32[]{:S(2)}) %collective-permute-start.3) | collective-permute-done | bytes 786464 | tf_op jit(solution)/shard_map/ppermute | solution.py:15
  84.2 1.2 constant_dynamic-update-slice_fusion.15
  85.4 1.2 constant_dynamic-update-slice_fusion.14
  86.7 0.1 constant_dynamic-update-slice_fusion.13
  86.7 0.1 constant_dynamic-update-slice_fusion.12
  86.8 1.2 constant_dynamic-update-slice_fusion.11
  88.0 0.1 constant_dynamic-update-slice_fusion.10
  88.0 1.2 constant_dynamic-update-slice_fusion.9
  89.3 0.0 collective-permute-done.6
  89.3 0.1 constant_dynamic-update-slice_fusion.8
  89.3 1.2 constant_dynamic-update-slice_fusion.7
  90.6 1.2 constant_dynamic-update-slice_fusion.6
  91.8 0.1 constant_dynamic-update-slice_fusion.5
  91.8 0.0 copy-start.3
  91.8 0.1 constant_dynamic-update-slice_fusion.4
  91.9 0.0 copy-done
  91.9 0.1 constant_dynamic-update-slice_fusion.3
  92.0 0.1 constant_dynamic-update-slice_fusion.2
  92.0 1.2 constant_dynamic-update-slice_fusion.1
  93.3 0.1 constant_dynamic-update-slice_fusion
  93.3 0.0 copy-done.1
  93.3 0.0 copy-start.2
  93.4 2.7 %fusion.7 = f32[1536,384]{0,1:T(8,128)S(1)} fusion(bf16[384,2048]{1,0:T(8,128)(2,1)S(1)} %copy-done.1, bf16[3072,2048]{1,0:T(8,128)(2,1)S(1)} %constant_dynamic-update-slice_fusion, s32[]{:T(128)S(6)} %select_n.34, f32[384]{0:T(512)S(1)} %broadcast_multiply_fusion, f32[384]{0:T(512)S(1)} %select_reduce_fusion.1), kind=kOutput, calls=%fused_computation.6 | convolution fusion | flops 2417098752 | bytes 10227716 | tf_op jit(solution)/shard_map/dot_general | solution.py:37
  96.0 0.0 copy-done.3
  96.0 1.5 select_reduce_fusion
  97.6 0.4 copy-done.2
  97.9 13.9 %pmax.7 = f32[1536]{0:T(1024)S(1)} all-reduce(f32[1536]{0:T(1024)S(1)} %get-tuple-element.2), channel_id=1, replica_groups=mesh['img'=4,'tpl'=8] {'tpl'}, use_global_device_ids=true, to_apply=%region_3.4 | all-reduce | flops 1536 | bytes 12288 | tf_op jit(solution)/shard_map/pmax | solution.py:42
  111.8 0.6 fusion.12
  112.4 13.9 %psum.14 = f32[1536]{0:T(1024)S(1)} all-reduce(f32[1536]{0:T(1024)S(1)} %fusion.12), channel_id=1, replica_groups=mesh['img'=4,'tpl'=8] {'tpl'}, use_global_device_ids=true, to_apply=%region_5.6 | all-reduce | flops 1536 | bytes 12288 | tf_op jit(solution)/shard_map/psum | solution.py:44
  126.3 7.5 %fusion = f32[384,2048]{1,0:T(8,128)} fusion(bf16[3072,2048]{1,0:T(8,128)(2,1)} %copy-done.2, s32[]{:T(128)S(6)} %select_n.34, pred[1536,384]{0,1:T(32,128)(4,1)S(1)} %get-tuple-element.3, f32[1536,384]{0,1:T(8,128)S(1)} %fusion.7, f32[1536]{0:T(1024)S(1)} %psum.14, f32[1536]{0:T(1024)S(1)} %pmax.7), kind=kOutput, calls=%fused_computation | convolution fusion | flops 2418278400 | bytes 12398596 | tf_op jit(solution)/shard_map/dot_general | solution.py:48
  133.8 0.0 reduce-scatter.2.cloned.1.call-update
  133.8 0.7 fusion.14
  134.5 11.1 %psum.15 = f32[384]{0:T(512)S(1)} all-reduce(f32[384]{0:T(512)S(1)} %fusion.14), channel_id=1, replica_groups=mesh['img'=4,'tpl'=8] {'img'}, use_global_device_ids=true, to_apply=%region_8.9 | all-reduce | flops 384 | bytes 3072 | tf_op jit(solution)/shard_map/psum | solution.py:54
  145.6 0.6 log_add_fusion
  146.2 30.7 %reduce-scatter.2.cloned.1.call-done = f32[384,512]{1,0:T(8,128)} async-done(((f32[384,2048]{1,0:T(8,128)}), f32[384,512]{1,0:T(8,128)}) %reduce-scatter.2.cloned.1.call-update) | async-done | bytes 786448 | tf_op jit(solution)/shard_map/reduce_scatter | solution.py:53
  176.9 2.2 %add_divide_fusion = f32[384,512]{1,0:T(8,128)} fusion(f32[384,512]{1,0:T(8,128)} %reduce-scatter.2.cloned.1.call-done, f32[384]{0:T(512)S(1)} %broadcast_add_fusion, bf16[384,2048]{1,0:T(8,128)(2,1)} %param.5, s32[]{:T(128)S(6)} %select_n.37), kind=kLoop, calls=%fused_computation.14 | loop fusion | flops 589824 | bytes 1967620 | tf_op jit(solution)/shard_map/div | solution.py:56
  (3 shorter events, 0.0 us)
Async XLA Ops:
  7.2 84.7 %copy-start = (bf16[192,2048]{1,0:T(8,128)(2,1)S(1)}, bf16[192,2048]{1,0:T(8,128)(2,1)}, u32[]{:S(2)}) copy-start(bf16[192,2048]{1,0:T(8,128)(2,1)} %param.4) | copy-start | bytes 2359300
  7.2 169.7 %reduce-scatter.2.cloned.1.call-start = ((), (), s32[]{:S(2)}) async-start(), calls=%async_computation.1 | async-start | bytes 3932160 | tf_op jit(solution)/shard_map/reduce_scatter | solution.py:53
  7.2 14.5 %collective-permute-start = (bf16[192,2048]{1,0:T(8,128)(2,1)}, bf16[192,2048]{1,0:T(8,128)(2,1)S(1)}, u32[]{:S(2)}, u32[]{:S(2)}) collective-permute-start(bf16[192,2048]{1,0:T(8,128)(2,1)} %param.4), channel_id=1, source_target_pairs={{0,1},{1,2},{2,3},{3,4},{4,5},{5,6},{6,7},{7,0},{8,9},{9,10},{10,1... | collective-permute-start | bytes 2359304 | tf_op jit(solution)/shard_map/ppermute | solution.py:15
  21.7 20.7 %collective-permute-start.1 = (bf16[192,2048]{1,0:T(8,128)(2,1)S(1)}, bf16[192,2048]{1,0:T(8,128)(2,1)S(1)}, u32[]{:S(2)}, u32[]{:S(2)}) collective-permute-start(bf16[192,2048]{1,0:T(8,128)(2,1)S(1)} %collective-permute-done), channel_id=1, source_target_pairs={{0,1},{1,2},{2,3},{3,4},{4,5},{5,6},{6,7},{7,0},{8,9},{9,10},{10,1... | collective-permute-start | bytes 2359304 | tf_op jit(solution)/shard_map/ppermute | solution.py:15
  21.7 20.7 %collective-permute-start.4 = (bf16[192,2048]{1,0:T(8,128)(2,1)}, bf16[192,2048]{1,0:T(8,128)(2,1)S(1)}, u32[]{:S(2)}, u32[]{:S(2)}) collective-permute-start(bf16[192,2048]{1,0:T(8,128)(2,1)} %param.4), channel_id=1, source_target_pairs={{0,7},{1,0},{2,1},{3,2},{4,3},{5,4},{6,5},{7,6},{8,15},{9,8},{10,9... | collective-permute-start | bytes 2359304 | tf_op jit(solution)/shard_map/ppermute | solution.py:17
  42.4 21.0 %collective-permute-start.2 = (bf16[192,2048]{1,0:T(8,128)(2,1)S(1)}, bf16[192,2048]{1,0:T(8,128)(2,1)}, u32[]{:S(2)}, u32[]{:S(2)}) collective-permute-start(bf16[192,2048]{1,0:T(8,128)(2,1)S(1)} %collective-permute-done.1), channel_id=1, source_target_pairs={{0,1},{1,2},{2,3},{3,4},{4,5},{5,6},{6,7},{7,0},{8,9},{9,10},{10,1... | collective-permute-start | bytes 2359304 | tf_op jit(solution)/shard_map/ppermute | solution.py:15
  42.4 23.6 %collective-permute-start.5 = (bf16[192,2048]{1,0:T(8,128)(2,1)S(1)}, bf16[192,2048]{1,0:T(8,128)(2,1)}, u32[]{:S(2)}, u32[]{:S(2)}) collective-permute-start(bf16[192,2048]{1,0:T(8,128)(2,1)S(1)} %collective-permute-done.4), channel_id=1, source_target_pairs={{0,7},{1,0},{2,1},{3,2},{4,3},{5,4},{6,5},{7,6},{8,15},{9,8},{10,9... | collective-permute-start | bytes 2359304 | tf_op jit(solution)/shard_map/ppermute | solution.py:17
  63.4 20.8 %collective-permute-start.3 = (bf16[192,2048]{1,0:T(8,128)(2,1)}, bf16[192,2048]{1,0:T(8,128)(2,1)}, u32[]{:S(2)}, u32[]{:S(2)}) collective-permute-start(bf16[192,2048]{1,0:T(8,128)(2,1)} %collective-permute-done.2), channel_id=1, source_target_pairs={{0,1},{1,2},{2,3},{3,4},{4,5},{5,6},{6,7},{7,0},{8,9},{9,10},{10,1... | collective-permute-start | bytes 2359304 | tf_op jit(solution)/shard_map/ppermute | solution.py:15
  66.0 27.3 %copy-start.1 = (bf16[384,2048]{1,0:T(8,128)(2,1)S(1)}, bf16[384,2048]{1,0:T(8,128)(2,1)}, u32[]{:S(2)}) copy-start(bf16[384,2048]{1,0:T(8,128)(2,1)} %param.5) | copy-start | bytes 4718596
  66.0 23.2 %collective-permute-start.6 = (bf16[192,2048]{1,0:T(8,128)(2,1)}, bf16[192,2048]{1,0:T(8,128)(2,1)S(1)}, u32[]{:S(2)}, u32[]{:S(2)}) collective-permute-start(bf16[192,2048]{1,0:T(8,128)(2,1)} %collective-permute-done.5), channel_id=1, source_target_pairs={{0,7},{1,0},{2,1},{3,2},{4,3},{5,4},{6,5},{7,6},{8,15},{9,8},{10,9... | collective-permute-start | bytes 2359304 | tf_op jit(solution)/shard_map/ppermute | solution.py:17
  91.8 4.2 %copy-start.3 = (s32[1536,8]{0,1:T(8,128)S(1)}, s32[1536,8]{0,1:T(8,128)}, u32[]{:S(2)}) copy-start(s32[1536,8]{0,1:T(8,128)} %param.7) | copy-start | bytes 147460
  93.3 4.6 %copy-start.2 = (bf16[3072,2048]{1,0:T(8,128)(2,1)}, bf16[3072,2048]{1,0:T(8,128)(2,1)S(1)}, u32[]{:S(2)}) copy-start(bf16[3072,2048]{1,0:T(8,128)(2,1)S(1)} %constant_dynamic-update-slice_fusion) | copy-start | bytes 37748740
Sparse Core Ops, SparseCore 0:
  133.9 42.9 reduce-scatter.1
